TPU v7x, 512 devices: a whole 4x8x8 slice. The times are simulated.
512 devices in a mesh: row: 16 (over y, x_hi), col: 32 (over z, x_lo, core).
Axes of the slice: x: 4 (x_hi: 2, x_lo: 2; x = x_hi * 2 + x_lo), y: 8, z: 8, core: 2. Of those that a mesh axis runs over, the one named last changes fastest.
Arguments:
- features: bfloat16 [32, 2048, 128], P('col'), may hold values from -6 to 6
- dst_features: bfloat16 [65536, 128], P(('row', 'col')), may hold values from -6 to 6
- w_self: bfloat16 [128, 256], replicated, may hold values from -0.5 to 0.5
- w_neigh: bfloat16 [128, 256], replicated, may hold values from -0.5 to 0.5
- cotangent: bfloat16 [65536, 256], P(('row', 'col')), may hold values from -6 to 6
- block_values: bfloat16 [16, 32, 32, 128, 128], P('row', 'col'), may hold values from -0.15625 to 0.15625
- block_rows: int32 [16, 32, 32], P('row', 'col'), may hold values from 0 to 31, as said below
- block_cols: int32 [16, 32, 32], P('row', 'col'), may hold values from 0 to 15
- block_counts: int32 [16, 32], P('row', 'col'), may hold values from 4 to 32, as said below
Outputs:
- output: bfloat16 [65536, 256], P(('row', 'col'))
- grad_w_self: float32 [128, 256], replicated
- grad_w_neigh: float32 [128, 256], replicated
- grad_features: float32 [32, 2048, 128], P('col', 'row')
Inputs may be any that keep to these rules, and one draw needn't show every extreme that they name: On one device the slots name distinct pairs of block_rows and block_cols, also in unused slots. `block_counts`: some device uses all 32 slots in every draw.
All inputs are finite; a program needn't handle non-finite values.
Results may differ from a plain program's by a relative error of at most 0.0052.
Values may be sent and summed in bfloat16 or wider, within the bound.
A program may use at most 64 MiB of HBM per device.

v0:
```python
import math
import jax
import jax.numpy as jnp
from jax import lax
from jax.sharding import PartitionSpec as P


def slot_products(block_vals, source_table, slot_index, einsum_form):
    return jnp.einsum(
        einsum_form, block_vals, source_table[slot_index], preferred_element_type=jnp.float32
    )


def per_device(
    features,
    dst_features,
    w_self,
    w_neigh,
    cotangent,
    block_values,
    block_rows,
    block_cols,
    block_counts,
):
    block_size = block_values.shape[-1]
    feat_width = features.shape[-1]
    local_rows = dst_features.shape[0]
    col_total = lax.axis_size("col")
    slab_blocks = local_rows * col_total // block_size
    source_table = features.reshape(-1, block_size, feat_width)
    source_count = source_table.shape[0]
    block_vals = block_values[0, 0]
    row_ids = block_rows[0, 0]
    col_ids = block_cols[0, 0]
    live_count = block_counts[0, 0]
    slot_total = row_ids.shape[0]
    live_mask = jnp.arange(slot_total, dtype=jnp.int32) < live_count
    row_hits = (
        (row_ids[None, :] == jnp.arange(slab_blocks, dtype=jnp.int32)[:, None]) & live_mask[None, :]
    ).astype(jnp.float32)
    forward_terms = slot_products(block_vals, source_table, col_ids, "sij,sjf->sif")
    summed = jnp.einsum("rs,sif->rif", row_hits, forward_terms, precision=lax.Precision.HIGHEST)
    agg_sum = lax.psum_scatter(
        summed.reshape(local_rows * lax.axis_size("col"), feat_width),
        "col",
        scatter_dimension=0,
        tiled=True,
    )
    aggregate = agg_sum.astype(jnp.bfloat16)
    pre_act = jnp.dot(dst_features, w_self, preferred_element_type=jnp.float32) + jnp.dot(
        aggregate, w_neigh, preferred_element_type=jnp.float32
    )
    sigmoid_pre = jax.nn.sigmoid(pre_act)
    output = (pre_act * sigmoid_pre).astype(jnp.bfloat16)
    grad_pre = (
        cotangent.astype(jnp.float32) * sigmoid_pre * (1.0 + pre_act * (1.0 - sigmoid_pre))
    ).astype(jnp.bfloat16)
    node_total = local_rows * lax.axis_size("row") * col_total
    scale_factor = 1.0 / math.sqrt(node_total)
    self_grad = jnp.einsum("nf,nh->fh", dst_features, grad_pre, preferred_element_type=jnp.float32)
    neigh_grad = jnp.einsum("nf,nh->fh", aggregate, grad_pre, preferred_element_type=jnp.float32)
    self_sum, neigh_sum = lax.psum((self_grad, neigh_grad), ("row", "col"))
    local_grad = jnp.einsum(
        "nh,fh->nf", grad_pre, w_neigh, preferred_element_type=jnp.float32
    ).astype(jnp.bfloat16)
    slab_grad = lax.all_gather(local_grad, "col", axis=0, tiled=True)
    grad_table = slab_grad.reshape(slab_blocks, block_size, feat_width)
    backward_terms = slot_products(block_vals, grad_table, row_ids, "sij,sif->sjf")
    col_hits = (
        (col_ids[None, :] == jnp.arange(source_count, dtype=jnp.int32)[:, None])
        & live_mask[None, :]
    ).astype(jnp.float32)
    source_terms = jnp.einsum(
        "cs,sjf->cjf", col_hits, backward_terms, precision=lax.Precision.HIGHEST
    ).reshape(-1, feat_width)
    source_part = lax.psum_scatter(source_terms, "row", scatter_dimension=0, tiled=True)
    return (
        output,
        self_sum * scale_factor,
        neigh_sum * scale_factor,
        source_part.reshape(1, -1, feat_width),
    )


def solution(mesh):
    placed = (
        P("col", None, None),
        P(("row", "col"), None),
        P(),
        P(),
        P(("row", "col"), None),
        P("row", "col", None, None, None),
        P("row", "col", None),
        P("row", "col", None),
        P("row", "col"),
    )
    return jax.shard_map(
        per_device,
        mesh=mesh,
        in_specs=placed,
        out_specs=(P(("row", "col"), None), P(), P(), P("col", "row", None)),
        check_vma=False,
    )
```

profile of v0, /device:TPU:16, one launch (start us, length us, event | category | flops | bytes accessed | tf_op | source)
XLA Modules:
  0.0 701.7 jit_solution(4395809418823105912)
XLA Ops:
  7.2 0.0 copy-start
  7.2 0.0 reduce-scatter.3.cloned.1.call-start
  8.0 0.7 fusion.21
  8.6 1.8 gather_fusion
  10.4 0.0 copy-done
  10.4 2.2 fusion.6
  12.7 0.0 copy-start.4
  12.7 2.4 copy.21
  15.1 0.0 copy-done.4
  15.1 1.1 fusion.2
  16.2 2.6 copy.16
  18.8 0.0 copy-start.1
  18.8 0.0 copy-start.2
  18.8 0.0 copy-start.3
  18.8 0.0 copy-start.6
  18.8 0.0 reduce-scatter.3.cloned.1.call-update
  18.8 0.0 all-gather.2.cloned.1.call-start
  18.8 0.7 copy-done.1
  19.5 0.1 copy-done.2
  19.6 0.1 fusion.23
  19.8 125.8 %reduce-scatter.3.cloned.1.call-done = f32[128,128]{1,0:T(8,128)} async-done(((f32[4096,128]{1,0:T(8,128)}), f32[128,128]{1,0:T(8,128)}) %reduce-scatter.3.cloned.1.call-update) | async-done | bytes 65552 | tf_op jit(solution)/shard_map/reduce_scatter | solution.py:43
  145.6 0.0 copy-done.3
  145.6 0.0 copy-done.6
  145.6 1.7 multiply_convert_fusion
  147.2 0.8 convolution_convert_fusion
  148.0 0.0 all-gather.2.cloned.1.call-update
  148.0 0.0 all-reduce.3.cloned.1.call-start
  148.1 0.8 convolution_bitcast_fusion
  149.0 1.7 fusion.8
  150.7 0.0 all-reduce.3.cloned.1.call-update
  150.7 0.0 reduce-scatter.5.cloned.1.call-start
  150.8 61.6 %all-gather.2.cloned.1.call-done = bf16[4096,128]{1,0:T(8,128)(2,1)} async-done(((bf16[128,128]{1,0:T(8,128)(2,1)}), bf16[4096,128]{1,0:T(8,128)(2,1)}) %all-gather.2.cloned.1.call-update) | async-done | bytes 1048592 | tf_op jit(solution)/shard_map/all_gather | solution.py:66
  212.3 2.0 gather_fusion.1
  214.3 1.9 fusion.4
  216.2 0.0 copy-start.5
  216.2 2.4 copy.23
  218.6 0.0 copy-done.5
  218.6 0.8 fusion
  219.4 1.3 copy.18
  220.7 0.0 reduce-scatter.5.cloned.1.call-update
  220.8 265.3 %all-reduce.3.cloned.1.call-done = (f32[128,256]{0,1:T(8,128)}, f32[128,256]{0,1:T(8,128)}) async-done(((f32[128,256]{0,1:T(8,128)}, f32[128,256]{0,1:T(8,128)}), (f32[128,256]{0,1:T(8,128)}, f32[128,256]{0,1:T(8,128)})) %all-reduce.3.cloned.1.call-update) | async-done | bytes 262160 | tf_op jit(solution)/shard_map/psum | solution.py:62
  486.1 1.0 broadcast_multiply_fusion
  487.1 0.8 copy.20
  487.8 0.8 copy.19
  488.6 206.6 %reduce-scatter.5.cloned.1.call-done = f32[128,128]{1,0:T(8,128)} async-done(((f32[2048,128]{1,0:T(8,128)}), f32[128,128]{1,0:T(8,128)}) %reduce-scatter.5.cloned.1.call-update) | async-done | bytes 65552 | tf_op jit(solution)/shard_map/reduce_scatter | solution.py:76
  (4 shorter events, 0.0 us)
Async XLA Ops:
  7.2 3.3 copy-start
  7.2 138.4 %reduce-scatter.3.cloned.1.call-start = ((), (), s32[]{:S(2)}) async-start(), calls=%async_computation.2 | async-start | bytes 2162688 | tf_op jit(solution)/shard_map/reduce_scatter | solution.py:43
  12.7 2.4 copy-start.4
  18.8 0.8 copy-start.1
  18.8 0.9 copy-start.2
  18.8 126.8 %copy-start.3 = (bf16[128,256]{1,0:T(8,128)(2,1)S(1)}, bf16[128,256]{1,0:T(8,128)(2,1)}, u32[]{:S(2)}) copy-start(bf16[128,256]{1,0:T(8,128)(2,1)} %param.12) | copy-start | bytes 196612
  18.8 126.8 %copy-start.6 = (bf16[128,256]{1,0:T(8,128)(2,1)S(1)}, bf16[128,256]{1,0:T(8,128)(2,1)}, u32[]{:S(2)}) copy-start(bf16[128,256]{1,0:T(8,128)(2,1)} %param.13) | copy-start | bytes 196612
  18.8 193.5 %all-gather.2.cloned.1.call-start = ((), (), s32[]{:S(2)}) async-start(), calls=%async_computation.3 | async-start | bytes 1081344 | tf_op jit(solution)/shard_map/all_gather | solution.py:66
  148.0 338.1 %all-reduce.3.cloned.1.call-start = ((), (), s32[]{:S(2)}) async-start(), calls=%async_computation.5 | async-start | bytes 524288 | tf_op jit(solution)/shard_map/psum | solution.py:62
  150.7 544.5 %reduce-scatter.5.cloned.1.call-start = ((), (), s32[]{:S(2)}) async-start(), calls=%async_computation.4 | async-start | bytes 1114112 | tf_op jit(solution)/shard_map/reduce_scatter | solution.py:76
  216.2 2.4 copy-start.5
Sparse Core Ops, SparseCore 0:
  18.9 126.5 reduce-scatter.2
  148.5 63.7 all-gather.1
  218.9 267.1 all-reduce.2
  490.9 204.2 reduce-scatter.4
where the time goes:
time: 702 us
  waiting for transfers between devices  659 us (94%)
  local copies, waits for them, and re-layouts  14.7 us (2%)
  between operations  14.6 us (2%)
  matrix products  11.2 us (2%)
    psum x1, waiting for transfers between devices, per_device(): self_sum, neigh_sum = lax.psum((self_grad, neigh_grad), ('row', 'col'))  265 us
    reduce_scatter x1, waiting for transfers between devices, per_device(): lax.psum_scatter(source_terms, 'row', scatter_dimension=0, tiled=True)  207 us
    reduce_scatter x1, waiting for transfers between devices, per_device(): lax.psum_scatter(summed.reshape(local_rows * lax.axis_size('col'), feat_w...  126 us
    all_gather x1, waiting for transfers between devices, per_device(): slab_grad = lax.all_gather(local_grad, 'col', axis=0, tiled=True)  61.6 us
  transfers between devices with their start and end apart: 4, of which 4 were waited for; matrix products, arithmetic and copies ran while one was open for 2% of the time, Pallas kernels for 0%

commit v1 on v0

--- a/solution.py
+++ b/solution.py
@@ -1,8 +1,18 @@
+import functools
 import math
 import jax
 import jax.numpy as jnp
 from jax import lax
 from jax.sharding import PartitionSpec as P
+
+
+def _treat_frame(u, dev_axis, which_axis):
+    for num in (dev_axis, which_axis):
+        u = lax.psum(u, num)
+    return u
+
+
+bands_watch = functools.partial(_treat_frame, dev_axis="col", which_axis="row")
 
 
 def slot_products(block_vals, source_table, slot_index, einsum_form):
@@ -59,7 +69,7 @@
     scale_factor = 1.0 / math.sqrt(node_total)
     self_grad = jnp.einsum("nf,nh->fh", dst_features, grad_pre, preferred_element_type=jnp.float32)
     neigh_grad = jnp.einsum("nf,nh->fh", aggregate, grad_pre, preferred_element_type=jnp.float32)
-    self_sum, neigh_sum = lax.psum((self_grad, neigh_grad), ("row", "col"))
+    self_sum, neigh_sum = bands_watch((self_grad, neigh_grad))
     local_grad = jnp.einsum(
         "nh,fh->nf", grad_pre, w_neigh, preferred_element_type=jnp.float32
     ).astype(jnp.bfloat16)

time: 702 us -> 829 us (1.18)
  waiting for transfers between devices: 659 us -> 786 us
    psum x1 -> x2, waiting for transfers between devices: 265 us -> 380 us  [_treat_frame(): u = lax.psum(u, num)]
  transfers between devices with their start and end apart: 4 -> 5, of which waited for: 4 -> 5; matrix products, arithmetic and copies ran while one was open for 2% -> 1% of each run, Pallas kernels for 0% -> 0%
where the time goes in v1:
time: 829 us
  waiting for transfers between devices  786 us (95%)
  local copies, waits for them, and re-layouts  14.7 us (2%)
  between operations  14.6 us (2%)
  matrix products  11.2 us (1%)
    psum x2, waiting for transfers between devices, _treat_frame(): u = lax.psum(u, num)  380 us
    reduce_scatter x1, waiting for transfers between devices, per_device(): lax.psum_scatter(source_terms, 'row', scatter_dimension=0, tiled=True)  211 us
    reduce_scatter x1, waiting for transfers between devices, per_device(): lax.psum_scatter(summed.reshape(local_rows * lax.axis_size('col'), feat_w...  126 us
    all_gather x1, waiting for transfers between devices, per_device(): slab_grad = lax.all_gather(local_grad, 'col', axis=0, tiled=True)  69.5 us
  transfers between devices with their start and end apart: 5, of which 5 were waited for; matrix products, arithmetic and copies ran while one was open for 1% of the time, Pallas kernels for 0%

profile of v1, /device:TPU:16, one launch (start us, length us, event | category | flops | bytes accessed | tf_op | source)
XLA Modules:
  0.0 828.7 jit_solution(3565755258656175561)
XLA Ops:
  7.2 0.0 copy-start
  7.2 0.0 reduce-scatter.3.cloned.1.call-start
  8.0 0.7 fusion.21
  8.6 1.8 gather_fusion
  10.4 0.0 copy-done
  10.4 2.2 fusion.6
  12.7 0.0 copy-start.4
  12.7 2.4 copy.21
  15.0 0.0 copy-done.4
  15.1 1.1 fusion.2
  16.2 2.5 copy.16
  18.7 0.0 copy-start.1
  18.7 0.0 copy-start.2
  18.7 0.0 copy-start.3
  18.8 0.0 copy-start.6
  18.8 0.0 reduce-scatter.3.cloned.1.call-update
  18.8 0.0 all-reduce.5.cloned.1.call-start
  18.8 0.7 copy-done.1
  19.5 0.1 copy-done.2
  19.6 0.1 fusion.23
  19.7 125.8 %reduce-scatter.3.cloned.1.call-done = f32[128,128]{1,0:T(8,128)} async-done(((f32[4096,128]{1,0:T(8,128)}), f32[128,128]{1,0:T(8,128)}) %reduce-scatter.3.cloned.1.call-update) | async-done | bytes 65552 | tf_op jit(solution)/shard_map/reduce_scatter | solution.py:53
  145.5 0.0 copy-done.3
  145.5 0.0 copy-done.6
  145.5 1.7 multiply_convert_fusion
  147.2 0.8 convolution_bitcast_fusion
  148.1 1.7 fusion.8
  149.8 0.0 all-reduce.5.cloned.1.call-update
  149.8 0.0 all-gather.2.cloned.1.call-start
  149.9 0.8 convolution_convert_fusion
  150.6 0.0 all-gather.2.cloned.1.call-update
  150.7 0.0 all-reduce.7.cloned.1.call-start
  150.7 225.0 %all-reduce.5.cloned.1.call-done = (f32[128,256]{0,1:T(8,128)}, f32[128,256]{0,1:T(8,128)}) async-done(((f32[128,256]{0,1:T(8,128)}, f32[128,256]{0,1:T(8,128)}), (f32[128,256]{0,1:T(8,128)}, f32[128,256]{0,1:T(8,128)})) %all-reduce.5.cloned.1.call-update) | async-done | bytes 262160 | tf_op jit(solution)/shard_map/psum | solution.py:11
  375.7 0.0 all-reduce.7.cloned.1.call-update
  375.7 0.0 reduce-scatter.5.cloned.1.call-start
  375.8 69.5 %all-gather.2.cloned.1.call-done = bf16[4096,128]{1,0:T(8,128)(2,1)} async-done(((bf16[128,128]{1,0:T(8,128)(2,1)}), bf16[4096,128]{1,0:T(8,128)(2,1)}) %all-gather.2.cloned.1.call-update) | async-done | bytes 1048592 | tf_op jit(solution)/shard_map/all_gather | solution.py:76
  445.3 2.0 gather_fusion.1
  447.3 1.9 fusion.4
  449.1 0.0 copy-start.5
  449.1 2.4 copy.23
  451.5 0.0 copy-done.5
  451.5 0.8 fusion
  452.4 1.3 copy.18
  453.7 0.0 reduce-scatter.5.cloned.1.call-update
  453.7 155.3 %all-reduce.7.cloned.1.call-done = (f32[128,256]{0,1:T(8,128)}, f32[128,256]{0,1:T(8,128)}) async-done(((f32[128,256]{0,1:T(8,128)}, f32[128,256]{0,1:T(8,128)}), (f32[128,256]{0,1:T(8,128)}, f32[128,256]{0,1:T(8,128)})) %all-reduce.7.cloned.1.call-update) | async-done | bytes 262160 | tf_op jit(solution)/shard_map/psum | solution.py:11
  609.0 1.0 broadcast_multiply_fusion
  609.9 0.8 copy.20
  610.7 0.8 copy.19
  611.5 210.7 %reduce-scatter.5.cloned.1.call-done = f32[128,128]{1,0:T(8,128)} async-done(((f32[2048,128]{1,0:T(8,128)}), f32[128,128]{1,0:T(8,128)}) %reduce-scatter.5.cloned.1.call-update) | async-done | bytes 65552 | tf_op jit(solution)/shard_map/reduce_scatter | solution.py:86
  (4 shorter events, 0.0 us)
Async XLA Ops:
  7.2 3.3 copy-start
  7.2 138.4 %reduce-scatter.3.cloned.1.call-start = ((), (), s32[]{:S(2)}) async-start(), calls=%async_computation.2 | async-start | bytes 2162688 | tf_op jit(solution)/shard_map/reduce_scatter | solution.py:53
  12.7 2.4 copy-start.4
  18.7 0.8 copy-start.1
  18.7 0.9 copy-start.2
  18.7 126.8 %copy-start.3 = (bf16[128,256]{1,0:T(8,128)(2,1)S(1)}, bf16[128,256]{1,0:T(8,128)(2,1)}, u32[]{:S(2)}) copy-start(bf16[128,256]{1,0:T(8,128)(2,1)} %param.12) | copy-start | bytes 196612
  18.8 126.8 %copy-start.6 = (bf16[128,256]{1,0:T(8,128)(2,1)S(1)}, bf16[128,256]{1,0:T(8,128)(2,1)}, u32[]{:S(2)}) copy-start(bf16[128,256]{1,0:T(8,128)(2,1)} %param.13) | copy-start | bytes 196612
  18.8 356.9 %all-reduce.5.cloned.1.call-start = ((), (), s32[]{:S(2)}) async-start(), calls=%async_computation.5 | async-start | bytes 524288 | tf_op jit(solution)/shard_map/psum | solution.py:11
  149.8 295.5 %all-gather.2.cloned.1.call-start = ((), (), s32[]{:S(2)}) async-start(), calls=%async_computation.3 | async-start | bytes 1081344 | tf_op jit(solution)/shard_map/all_gather | solution.py:76
  150.7 458.3 %all-reduce.7.cloned.1.call-start = ((), (), s32[]{:S(2)}) async-start(), calls=%async_computation.6 | async-start | bytes 524288 | tf_op jit(solution)/shard_map/psum | solution.py:11
  375.7 446.4 %reduce-scatter.5.cloned.1.call-start = ((), (), s32[]{:S(2)}) async-start(), calls=%async_computation.4 | async-start | bytes 1114112 | tf_op jit(solution)/shard_map/reduce_scatter | solution.py:86
  449.1 2.4 copy-start.5
Sparse Core Ops, SparseCore 0:
  18.9 126.5 reduce-scatter.2
  149.9 225.7 all-reduce.4
  378.4 66.7 all-gather.1
  448.1 160.8 all-reduce.6
  614.4 207.6 reduce-scatter.4

commit v2 on v0

--- a/solution.py
+++ b/solution.py
@@ -1,8 +1,20 @@
+import functools
 import math
 import jax
 import jax.numpy as jnp
 from jax import lax
 from jax.sharding import PartitionSpec as P
+from jax.lax import all_to_all, axis_size
+
+
+def load_the_lanes(inputs, device_axis, join_dim):
+    local_out = jnp.concatenate(
+        all_to_all(jnp.stack([inputs] * axis_size(device_axis)), device_axis, 0, 0), axis=join_dim
+    )
+    return local_out
+
+
+_read_sections = functools.partial(load_the_lanes, device_axis="col", join_dim=0)
 
 
 def slot_products(block_vals, source_table, slot_index, einsum_form):
@@ -63,7 +75,7 @@
     local_grad = jnp.einsum(
         "nh,fh->nf", grad_pre, w_neigh, preferred_element_type=jnp.float32
     ).astype(jnp.bfloat16)
-    slab_grad = lax.all_gather(local_grad, "col", axis=0, tiled=True)
+    slab_grad = _read_sections(local_grad)
     grad_table = slab_grad.reshape(slab_blocks, block_size, feat_width)
     backward_terms = slot_products(block_vals, grad_table, row_ids, "sij,sif->sjf")
     col_hits = (

time: 702 us -> 645 us (0.919)
  waiting for transfers between devices: 659 us -> 600 us
    all_gather x1 -> x0, waiting for transfers between devices: 61.6 us -> none  [per_device(): slab_grad = lax.all_gather(local_grad, 'col', axis=0, tiled=True)]
    all_to_all x0 -> x1, waiting for transfers between devices: none -> 27.3 us  [load_the_lanes(): all_to_all(jnp.stack([inputs] * axis_size(device_axis)), device_axis, 0, 0)]
    psum x1, waiting for transfers between devices: 265 us -> 240 us  [per_device(): self_sum, neigh_sum = lax.psum((self_grad, neigh_grad), ('row', 'col'))]
where the time goes in v2:
time: 645 us
  waiting for transfers between devices  600 us (93%)
  local copies, waits for them, and re-layouts  14.8 us (2%)
  between operations  14.6 us (2%)
  matrix products  9.82 us (2%)
    psum x1, waiting for transfers between devices, per_device(): self_sum, neigh_sum = lax.psum((self_grad, neigh_grad), ('row', 'col'))  240 us
    reduce_scatter x1, waiting for transfers between devices, per_device(): lax.psum_scatter(source_terms, 'row', scatter_dimension=0, tiled=True)  207 us
    reduce_scatter x1, waiting for transfers between devices, per_device(): lax.psum_scatter(summed.reshape(local_rows * lax.axis_size('col'), feat_w...  126 us
    all_to_all x1, waiting for transfers between devices, load_the_lanes(): all_to_all(jnp.stack([inputs] * axis_size(device_axis)), device_axis, 0, 0)  27.3 us
  transfers between devices with their start and end apart: 4, of which 4 were waited for; matrix products, arithmetic and copies ran while one was open for 2% of the time, Pallas kernels for 0%

profile of v2, /device:TPU:16, one launch (start us, length us, event | category | flops | bytes accessed | tf_op | source)
XLA Modules:
  0.0 644.7 jit_solution(5515891633217700515)
XLA Ops:
  7.2 0.0 copy-start
  7.2 0.0 reduce-scatter.3.cloned.1.call-start
  8.0 0.7 fusion.21
  8.6 1.8 gather_fusion
  10.4 0.0 copy-done
  10.4 2.2 fusion.6
  12.7 0.0 copy-start.5
  12.7 2.4 copy.21
  15.1 0.0 copy-done.5
  15.1 1.1 fusion.2
  16.2 2.6 copy.16
  18.8 0.0 copy-start.1
  18.8 0.0 copy-start.2
  18.8 0.0 copy-start.3
  18.8 0.0 copy-start.7
  18.8 0.0 reduce-scatter.3.cloned.1.call-update
  18.8 0.7 copy-done.1
  19.5 0.1 copy-done.2
  19.6 0.1 fusion.23
  19.8 125.8 %reduce-scatter.3.cloned.1.call-done = f32[128,128]{1,0:T(8,128)} async-done(((f32[4096,128]{1,0:T(8,128)}), f32[128,128]{1,0:T(8,128)}) %reduce-scatter.3.cloned.1.call-update) | async-done | bytes 65552 | tf_op jit(solution)/shard_map/reduce_scatter | solution.py:55
  145.6 0.0 copy-done.3
  145.6 0.0 copy-done.7
  145.6 0.0 copy-start.4
  145.6 1.7 multiply_convert_fusion
  147.3 0.2 convolution_convert_fusion
  147.5 1.2 stack.2
  148.7 4.1 all-to-all-start
  152.9 0.0 all-reduce.3.cloned.1.call-start
  152.9 0.9 convolution_bitcast_fusion
  153.8 0.0 copy-done.4
  153.8 0.9 fusion.8
  154.7 0.0 all-reduce.3.cloned.1.call-update
  154.7 0.0 reduce-scatter.5.cloned.1.call-start
  154.7 27.3 %all-to-all-done = bf16[32,128,128]{2,1,0:T(8,128)(2,1)S(1)} async-done(((bf16[32,128,128]{2,1,0:T(8,128)(2,1)}), bf16[32,128,128]{2,1,0:T(8,128)(2,1)S(1)}, u32[]{:S(2)}, u32[]{:S(2)}) %all-to-all-start) | async-done | bytes 1048608 | tf_op jit(solution)/shard_map/all_to_all | solution.py:12
  182.0 0.7 gather_fusion.1
  182.8 1.9 fusion.4
  184.7 0.0 copy-start.6
  184.7 2.4 copy.23
  187.0 0.0 copy-done.6
  187.1 0.8 fusion
  187.9 1.3 copy.18
  189.2 0.0 reduce-scatter.5.cloned.1.call-update
  189.2 239.7 %all-reduce.3.cloned.1.call-done = (f32[128,256]{0,1:T(8,128)}, f32[128,256]{0,1:T(8,128)}) async-done(((f32[128,256]{0,1:T(8,128)}, f32[128,256]{0,1:T(8,128)}), (f32[128,256]{0,1:T(8,128)}, f32[128,256]{0,1:T(8,128)})) %all-reduce.3.cloned.1.call-update) | async-done | bytes 262160 | tf_op jit(solution)/shard_map/psum | solution.py:74
  428.9 1.0 broadcast_multiply_fusion
  429.9 0.8 copy.20
  430.7 0.8 copy.19
  431.4 206.7 %reduce-scatter.5.cloned.1.call-done = f32[128,128]{1,0:T(8,128)} async-done(((f32[2048,128]{1,0:T(8,128)}), f32[128,128]{1,0:T(8,128)}) %reduce-scatter.5.cloned.1.call-update) | async-done | bytes 65552 | tf_op jit(solution)/shard_map/reduce_scatter | solution.py:88
  (4 shorter events, 0.0 us)
Async XLA Ops:
  7.2 3.3 copy-start
  7.2 138.4 %reduce-scatter.3.cloned.1.call-start = ((), (), s32[]{:S(2)}) async-start(), calls=%async_computation.3 | async-start | bytes 2162688 | tf_op jit(solution)/shard_map/reduce_scatter | solution.py:55
  12.7 2.4 copy-start.5
  18.8 0.8 copy-start.1
  18.8 0.9 copy-start.2
  18.8 126.8 %copy-start.3 = (bf16[128,256]{1,0:T(8,128)(2,1)S(1)}, bf16[128,256]{1,0:T(8,128)(2,1)}, u32[]{:S(2)}) copy-start(bf16[128,256]{1,0:T(8,128)(2,1)} %param.12) | copy-start | bytes 196612
  18.8 126.8 %copy-start.7 = (bf16[128,256]{1,0:T(8,128)(2,1)S(1)}, bf16[128,256]{1,0:T(8,128)(2,1)}, u32[]{:S(2)}) copy-start(bf16[128,256]{1,0:T(8,128)(2,1)} %param.13) | copy-start | bytes 196612
  145.6 8.2 %copy-start.4 = (f32[128,128]{1,0:T(8,128)S(1)}, f32[128,128]{1,0:T(8,128)}, u32[]{:S(2)}) copy-start(f32[128,128]{1,0:T(8,128)} %reduce-scatter.3.cloned.1.call-done) | copy-start | bytes 196612
  148.7 33.3 %all-to-all-start = ((bf16[32,128,128]{2,1,0:T(8,128)(2,1)}), bf16[32,128,128]{2,1,0:T(8,128)(2,1)S(1)}, u32[]{:S(2)}, u32[]{:S(2)}) async-start(bf16[32,128,128]{2,1,0:T(8,128)(2,1)} %stack.2), calls=%async_computation.1 | async-start | bytes 2097152 | tf_op jit(solution)/shard_map/all_to_all | solution.py:12
  152.9 276.1 %all-reduce.3.cloned.1.call-start = ((), (), s32[]{:S(2)}) async-start(), calls=%async_computation.5 | async-start | bytes 524288 | tf_op jit(solution)/shard_map/psum | solution.py:74
  154.7 483.5 %reduce-scatter.5.cloned.1.call-start = ((), (), s32[]{:S(2)}) async-start(), calls=%async_computation.4 | async-start | bytes 1114112 | tf_op jit(solution)/shard_map/reduce_scatter | solution.py:88
  184.7 2.4 copy-start.6
Sparse Core Ops, SparseCore 0:
  18.9 126.6 reduce-scatter.2
  160.3 268.6 all-reduce.2
  433.9 204.1 reduce-scatter.4
